TPU v7x, 1024 devices: a whole 4x8x16 slice. The times are simulated.
1024 devices in a mesh: grp: 32 (over z, x_lo), dom: 32 (over x_hi, y, core).
Axes of the slice: x: 4 (x_hi: 2, x_lo: 2; x = x_hi * 2 + x_lo), y: 8, z: 16, core: 2. Of those that a mesh axis runs over, the one named last changes fastest.
Arguments:
- density: float32 [32, 256, 16384], P('grp', 'dom'), may hold values from -6 to 6
- diffusion: float32 [32, 256, 16384], P('grp', 'dom'), may hold values from 0.05 to 0.22
- drift_speed: float32 [32, 256, 16384], P('grp', 'dom'), may hold values from -0.3 to 0.3
- levels: int32 [32], P('grp'), may hold values from 5 to 8
- coefficient: int32 [32], P('grp'), may hold values from -2 to 2
Outputs:
- combined_field: float32 [32, 256, 16384], P('grp', 'dom')
All inputs are finite; a program needn't handle non-finite values.
Results may differ from a plain program's by a relative error of at most 0.0003.
Values sent between devices are 32-bit elements; how exact they have to be, the bound alone decides.
A program may use at most 32 MiB of HBM per device.

v0:
```python
import jax
import jax.numpy as jnp
import numpy as np
from jax import lax
from jax.sharding import PartitionSpec as P

STEPS = 4


def extended(array, sides, width):
    for axis, dim in sides:
        devices, length = (lax.axis_size(axis), array.shape[dim])
        up = [(i, (i + 1) % devices) for i in range(devices - 1)]
        down = [(j, i) for i, j in up]
        last = lax.slice_in_dim(array, length - width, length, axis=dim)
        leading = lax.slice_in_dim(array, 0, width, axis=dim)
        before = lax.ppermute(last, axis, up)
        after = lax.ppermute(leading, axis, down)
        array = jnp.concatenate([before, array, after], axis=dim)
    return array


def hier_tables(size):
    to_surplus = np.zeros((size, size), dtype=np.float32)
    to_nodal = np.zeros((size, size), dtype=np.float32)
    node_level = np.zeros((size,), dtype=np.int32)
    depth = size.bit_length() - 1
    spots = np.arange(1, size + 1, dtype=np.float32)
    for index in range(size):
        position = index + 1
        to_surplus[index, index] = 1.0
        if position == size:
            node_level[index] = 0
            to_nodal[:, index] = spots / size
            continue
        stride = 1
        zeros_count = 0
        while position % (2 * stride) == 0:
            stride = stride * 2
            zeros_count = zeros_count + 1
        node_level[index] = depth - zeros_count
        to_nodal[:, index] = np.maximum(0.0, 1.0 - np.abs(spots - position) / stride)
        if position - stride > 0:
            to_surplus[index, position - stride - 1] -= 0.5
        if position + stride <= size:
            to_surplus[index, position + stride - 1] -= 0.5
    return (to_surplus, to_nodal, node_level)


def advance(state, diffuse, drifts, padded):
    above_cell = padded[2:, 1:-1]
    below_cell = padded[:-2, 1:-1]
    right_cell = padded[1:-1, 2:]
    left_cell = padded[1:-1, :-2]
    return (
        state
        + diffuse * (above_cell + below_cell + right_cell + left_cell - 4.0 * state)
        - 0.5 * drifts * (above_cell - below_cell)
    )


def on_device(density, diffusion, drift_speed, levels, coefficient):
    state = density[0]
    diffuse = diffusion[0]
    drifts = drift_speed[0]
    rows_all = state.shape[0] * lax.axis_size("dom")
    to_surplus, to_nodal, node_level = hier_tables(rows_all)
    to_surplus = jnp.asarray(to_surplus)
    to_nodal = jnp.asarray(to_nodal)
    node_level = jnp.asarray(node_level)
    for sweep in range(STEPS):
        padded = extended(state, (("dom", 0),), 1)
        padded = jnp.pad(padded, ((0, 0), (1, 1)))
        state = advance(state, diffuse, drifts, padded)
    poles = lax.all_to_all(state, "dom", split_axis=1, concat_axis=0, tiled=True)
    surplus = jnp.dot(
        to_surplus, poles, precision=lax.Precision.HIGHEST, preferred_element_type=jnp.float32
    )
    member_mask = (node_level <= levels[0]).astype(jnp.float32)[:, None]
    weighted = surplus * (member_mask * coefficient[0].astype(jnp.float32))
    total = lax.psum(weighted, "grp")
    nodal = jnp.dot(
        to_nodal,
        total * member_mask,
        precision=lax.Precision.HIGHEST,
        preferred_element_type=jnp.float32,
    )
    slabs = lax.all_to_all(nodal, "dom", split_axis=0, concat_axis=1, tiled=True)
    return slabs[None]


def solution(mesh):
    return jax.shard_map(
        on_device,
        mesh=mesh,
        in_specs=(
            P("grp", "dom", None),
            P("grp", "dom", None),
            P("grp", "dom", None),
            P("grp"),
            P("grp"),
        ),
        out_specs=P("grp", "dom", None),
        check_vma=False,
    )
```

profile of v0, /device:TPU:1, one launch (start us, length us, event | category | flops | bytes accessed | tf_op | source)
XLA Modules:
  0.0 398.0 jit_solution(5856497812033132400)
XLA Ops:
  6.5 0.0 copy-start.2
  6.5 0.0 copy-start.1
  6.5 0.0 copy-start
  6.5 1.4 slice_bitcast_fusion
  8.0 16.1 %collective-permute-start = (f32[1,16384]{1,0:T(1,128)S(1)}, f32[1,16384]{1,0:T(1,128)S(1)}, u32[]{:S(2)}, u32[]{:S(2)}) collective-permute-start(f32[1,16384]{1,0:T(1,128)S(1)} %get-tuple-element.12), channel_id=1, source_target_pairs={{1,0},{2,1},{3,2},{4,3},{5,4},{6,5},{7,6},{8,7},{9,8},{10,9},{11,1... | collective-permute-start | bytes 196616 | tf_op jit(solution)/shard_map/ppermute | solution.py:18
  24.0 1.9 collective-permute-start.1
  26.0 0.0 collective-permute-done
  26.0 1.3 collective-permute-done.1
  27.3 1.7 select_maximum_fusion.6
  28.9 0.0 copy-done.2
  28.9 0.0 copy-done.1
  28.9 0.0 copy-done
  28.9 0.5 fusion.17
  29.4 0.1 fusion.22
  29.5 2.0 collective-permute-start.2
  31.5 4.2 %collective-permute-start.3 = (f32[1,16384]{1,0:T(1,128)S(1)}, f32[1,16384]{1,0:T(1,128)S(1)}, u32[]{:S(2)}, u32[]{:S(2)}) collective-permute-start(f32[1,16384]{1,0:T(1,128)S(1)} %get-tuple-element.9), channel_id=1, source_target_pairs={{0,1},{1,2},{2,3},{3,4},{4,5},{5,6},{6,7},{7,8},{8,9},{9,10},{10,1... | collective-permute-start | bytes 196616 | tf_op jit(solution)/shard_map/ppermute | solution.py:17
  35.7 0.0 collective-permute-done.2
  35.7 1.3 collective-permute-done.3
  37.0 0.6 select_maximum_fusion.4
  37.7 0.5 fusion.13
  38.2 0.1 fusion.21
  38.2 1.9 collective-permute-start.4
  40.2 4.3 %collective-permute-start.5 = (f32[1,16384]{1,0:T(1,128)S(1)}, f32[1,16384]{1,0:T(1,128)S(1)}, u32[]{:S(2)}, u32[]{:S(2)}) collective-permute-start(f32[1,16384]{1,0:T(1,128)S(1)} %get-tuple-element.7), channel_id=1, source_target_pairs={{0,1},{1,2},{2,3},{3,4},{4,5},{5,6},{6,7},{7,8},{8,9},{9,10},{10,1... | collective-permute-start | bytes 196616 | tf_op jit(solution)/shard_map/ppermute | solution.py:17
  44.4 0.0 collective-permute-done.4
  44.5 1.3 collective-permute-done.5
  45.8 0.6 select_maximum_fusion.2
  46.4 0.5 fusion.9
  46.9 0.1 fusion.20
  47.0 1.9 collective-permute-start.6
  48.9 4.3 %collective-permute-start.7 = (f32[1,16384]{1,0:T(1,128)S(1)}, f32[1,16384]{1,0:T(1,128)S(1)}, u32[]{:S(2)}, u32[]{:S(2)}) collective-permute-start(f32[1,16384]{1,0:T(1,128)S(1)} %get-tuple-element.5), channel_id=1, source_target_pairs={{0,1},{1,2},{2,3},{3,4},{4,5},{5,6},{6,7},{7,8},{8,9},{9,10},{10,1... | collective-permute-start | bytes 196616 | tf_op jit(solution)/shard_map/ppermute | solution.py:17
  53.2 0.0 collective-permute-done.6
  53.2 1.3 collective-permute-done.7
  54.5 0.6 select_maximum_fusion
  55.1 1.3 fusion.5
  56.4 0.0 copy-start.5
  56.4 0.0 copy-start.4
  56.4 11.6 %all-to-all-start = ((f32[8,32,512]{2,0,1:T(8,128)}), f32[8,32,512]{2,0,1:T(8,128)S(1)}, u32[]{:S(2)}, u32[]{:S(2)}) async-start(f32[8,32,512]{2,0,1:T(8,128)} %bitcast.5), calls=%async_computation | async-start | bytes 1048576 | tf_op jit(solution)/shard_map/all_to_all | solution.py:75
  68.0 0.0 all-reduce.6.cloned.1.call-start
  69.3 0.0 copy-done.5
  69.3 16.7 %all-to-all-done = f32[8,32,512]{2,0,1:T(8,128)S(1)} async-done(((f32[8,32,512]{2,0,1:T(8,128)}), f32[8,32,512]{2,0,1:T(8,128)S(1)}, u32[]{:S(2)}, u32[]{:S(2)}) %all-to-all-start) | async-done | bytes 524320 | tf_op jit(solution)/shard_map/all_to_all | solution.py:75
  86.0 0.3 copy.9
  86.3 0.0 copy-start.3
  86.3 0.0 copy-done.4
  86.4 1.8 fusion
  88.2 0.0 all-reduce.6.cloned.1.call-update
  88.2 251.3 %all-reduce.6.cloned.1.call-done = f32[256,512]{0,1:T(8,128)} async-done(((f32[256,512]{0,1:T(8,128)}), f32[256,512]{0,1:T(8,128)}) %all-reduce.6.cloned.1.call-update) | async-done | bytes 524304 | tf_op jit(solution)/shard_map/psum | solution.py:81
  339.4 0.0 copy-done.3
  339.4 1.7 convolution_bitcast_fusion
  341.1 49.2 %all_to_all.35 = f32[32,8,512]{2,1,0:T(8,128)S(1)} all-to-all(f32[32,8,512]{2,1,0:T(8,128)S(1)} %convolution_bitcast_fusion), channel_id=1, replica_groups=mesh['grp'=32,'dom'=32] {'dom'}, dimensions={0} | all-to-all | bytes 1048576 | tf_op jit(solution)/shard_map/all_to_all | solution.py:88
  390.4 0.8 copy.14
  (2 shorter events, 0.0 us)
Async XLA Ops:
  6.5 22.4 %copy-start.2 = (f32[1,8,16384]{2,1,0:T(8,128)S(1)}, f32[1,8,16384]{2,1,0:T(8,128)}, u32[]{:S(2)}) copy-start(f32[1,8,16384]{2,1,0:T(8,128)} %param.8) | copy-start | bytes 1572868
  6.5 22.4 %copy-start.1 = (f32[1,8,16384]{2,1,0:T(8,128)S(1)}, f32[1,8,16384]{2,1,0:T(8,128)}, u32[]{:S(2)}) copy-start(f32[1,8,16384]{2,1,0:T(8,128)} %param.10) | copy-start | bytes 1572868
  6.5 22.4 %copy-start = (f32[1,8,16384]{2,1,0:T(8,128)S(1)}, f32[1,8,16384]{2,1,0:T(8,128)}, u32[]{:S(2)}) copy-start(f32[1,8,16384]{2,1,0:T(8,128)} %param.9) | copy-start | bytes 1572868
  8.0 18.0 %collective-permute-start = (f32[1,16384]{1,0:T(1,128)S(1)}, f32[1,16384]{1,0:T(1,128)S(1)}, u32[]{:S(2)}, u32[]{:S(2)}) collective-permute-start(f32[1,16384]{1,0:T(1,128)S(1)} %get-tuple-element.12), channel_id=1, source_target_pairs={{1,0},{2,1},{3,2},{4,3},{5,4},{6,5},{7,6},{8,7},{9,8},{10,9},{11,1... | collective-permute-start | bytes 196616 | tf_op jit(solution)/shard_map/ppermute | solution.py:18
  24.0 3.2 collective-permute-start.1
  29.5 6.2 %collective-permute-start.2 = (f32[1,16384]{1,0:T(1,128)S(1)}, f32[1,16384]{1,0:T(1,128)S(1)}, u32[]{:S(2)}, u32[]{:S(2)}) collective-permute-start(f32[1,16384]{1,0:T(1,128)S(1)} %get-tuple-element.10), channel_id=1, source_target_pairs={{1,0},{2,1},{3,2},{4,3},{5,4},{6,5},{7,6},{8,7},{9,8},{10,9},{11,1... | collective-permute-start | bytes 196616 | tf_op jit(solution)/shard_map/ppermute | solution.py:18
  31.5 5.5 %collective-permute-start.3 = (f32[1,16384]{1,0:T(1,128)S(1)}, f32[1,16384]{1,0:T(1,128)S(1)}, u32[]{:S(2)}, u32[]{:S(2)}) collective-permute-start(f32[1,16384]{1,0:T(1,128)S(1)} %get-tuple-element.9), channel_id=1, source_target_pairs={{0,1},{1,2},{2,3},{3,4},{4,5},{5,6},{6,7},{7,8},{8,9},{9,10},{10,1... | collective-permute-start | bytes 196616 | tf_op jit(solution)/shard_map/ppermute | solution.py:17
  38.2 6.2 %collective-permute-start.4 = (f32[1,16384]{1,0:T(1,128)S(1)}, f32[1,16384]{1,0:T(1,128)S(1)}, u32[]{:S(2)}, u32[]{:S(2)}) collective-permute-start(f32[1,16384]{1,0:T(1,128)S(1)} %get-tuple-element.8), channel_id=1, source_target_pairs={{1,0},{2,1},{3,2},{4,3},{5,4},{6,5},{7,6},{8,7},{9,8},{10,9},{11,1... | collective-permute-start | bytes 196616 | tf_op jit(solution)/shard_map/ppermute | solution.py:18
  40.2 5.6 %collective-permute-start.5 = (f32[1,16384]{1,0:T(1,128)S(1)}, f32[1,16384]{1,0:T(1,128)S(1)}, u32[]{:S(2)}, u32[]{:S(2)}) collective-permute-start(f32[1,16384]{1,0:T(1,128)S(1)} %get-tuple-element.7), channel_id=1, source_target_pairs={{0,1},{1,2},{2,3},{3,4},{4,5},{5,6},{6,7},{7,8},{8,9},{9,10},{10,1... | collective-permute-start | bytes 196616 | tf_op jit(solution)/shard_map/ppermute | solution.py:17
  47.0 6.2 %collective-permute-start.6 = (f32[1,16384]{1,0:T(1,128)S(1)}, f32[1,16384]{1,0:T(1,128)S(1)}, u32[]{:S(2)}, u32[]{:S(2)}) collective-permute-start(f32[1,16384]{1,0:T(1,128)S(1)} %get-tuple-element.6), channel_id=1, source_target_pairs={{1,0},{2,1},{3,2},{4,3},{5,4},{6,5},{7,6},{8,7},{9,8},{10,9},{11,1... | collective-permute-start | bytes 196616 | tf_op jit(solution)/shard_map/ppermute | solution.py:18
  48.9 5.6 %collective-permute-start.7 = (f32[1,16384]{1,0:T(1,128)S(1)}, f32[1,16384]{1,0:T(1,128)S(1)}, u32[]{:S(2)}, u32[]{:S(2)}) collective-permute-start(f32[1,16384]{1,0:T(1,128)S(1)} %get-tuple-element.5), channel_id=1, source_target_pairs={{0,1},{1,2},{2,3},{3,4},{4,5},{5,6},{6,7},{7,8},{8,9},{9,10},{10,1... | collective-permute-start | bytes 196616 | tf_op jit(solution)/shard_map/ppermute | solution.py:17
  56.4 12.9 %copy-start.5 = (s32[256]{0:T(256)S(1)}, s32[256]{0:T(256)}, u32[]{:S(2)}) copy-start(s32[256]{0:T(256)} %constant.16.clone) | copy-start | bytes 3076
  56.4 30.0 %copy-start.4 = (f32[256,256]{1,0:T(8,128)S(1)}, f32[256,256]{1,0:T(8,128)}, u32[]{:S(2)}) copy-start(f32[256,256]{1,0:T(8,128)} %constant.32) | copy-start | bytes 786436
  56.4 29.7 %all-to-all-start = ((f32[8,32,512]{2,0,1:T(8,128)}), f32[8,32,512]{2,0,1:T(8,128)S(1)}, u32[]{:S(2)}, u32[]{:S(2)}) async-start(f32[8,32,512]{2,0,1:T(8,128)} %bitcast.5), calls=%async_computation | async-start | bytes 1048576 | tf_op jit(solution)/shard_map/all_to_all | solution.py:75
  68.0 271.5 %all-reduce.6.cloned.1.call-start = ((), (), s32[]{:S(2)}) async-start(), calls=%async_computation.2 | async-start | bytes 1048576 | tf_op jit(solution)/shard_map/psum | solution.py:81
  86.3 253.1 %copy-start.3 = (f32[256,256]{1,0:T(8,128)S(1)}, f32[256,256]{1,0:T(8,128)}, u32[]{:S(2)}) copy-start(f32[256,256]{1,0:T(8,128)} %constant.15.clone) | copy-start | bytes 786436
Sparse Core Ops, SparseCore 0:
  88.3 251.1 all-reduce.5
where the time goes:
time: 399 us; the launch traced here: 398 us
  waiting for transfers between devices  273 us (68%)
  blocking collectives  49.2 us (12%)
  starting transfers between devices  48.2 us (12%)
  between operations  14.9 us (4%)
  other arithmetic  6.23 us (2%)
    psum x1, waiting for transfers between devices, on_device(): total = lax.psum(weighted, 'grp')  251 us
    all_to_all x1, blocking collectives, on_device(): lax.all_to_all(nodal, 'dom', split_axis=0, concat_axis=1, tiled=True)  49.2 us
    ppermute x4, starting transfers between devices, extended(): after = lax.ppermute(leading, axis, down)  21.9 us
    all_to_all x1, waiting for transfers between devices, on_device(): lax.all_to_all(state, 'dom', split_axis=1, concat_axis=0, tiled=True)  16.7 us
    ppermute x4, starting transfers between devices, extended(): before = lax.ppermute(last, axis, up)  14.7 us
    all_to_all x1, starting transfers between devices, on_device(): lax.all_to_all(state, 'dom', split_axis=1, concat_axis=0, tiled=True)  11.6 us
  transfers between devices with their start and end apart: 10, of which 6 were waited for; matrix products, arithmetic and copies ran while one was open for 0% of the time, Pallas kernels for 0%

commit v1 on v0

v1 whole, which is shorter than its diff:
```python
import jax
import jax.numpy as jnp
from jax import lax
from jax.experimental import pallas as pl
from jax.experimental.pallas import tpu as pltpu
from jax.sharding import PartitionSpec as P

MESH = pl.DeviceIdType.MESH
CHUNKS = 4
Z = 16
DOM = 32
EDGES = ((0, 6), (6, 10), (10, 14), (14, 18))
FAR_FIRST = (8, 7, 9, 6, 10, 5, 11, 4, 12, 3, 13, 2, 14, 1, 15)


def kernel(
    lev_ref, coef_ref, den_ref, dif_ref, dri_ref, out_ref,
    in_d, in_k, in_v, D, K, V, A, B, W, RX, PZ, RZ, G, H,
    load_sem, halo_send, halo_recv, xs, xr, zs, zr, gs, gr, xgs, xgr, hs, hr,
):
    grp = lax.axis_index("grp")
    dom = lax.axis_index("dom")
    z = grp // 2
    x = grp % 2
    xo = 1 - x
    has_up = dom > 0
    has_down = dom < DOM - 1
    peer_x = (z * 2 + xo, dom)

    def z_peer(k):
        return (((z + k) % Z) * 2 + x, dom)

    loads = [
        pltpu.make_async_copy(src, dst, load_sem.at[i])
        for i, (src, dst) in enumerate(((den_ref, in_d), (dif_ref, in_k), (dri_ref, in_v)))
    ]
    for load in loads:
        load.start()

    barrier = pltpu.get_barrier_semaphore()

    def greet(device):
        pl.semaphore_signal(barrier, inc=1, device_id=device, device_id_type=MESH)

    for k in FAR_FIRST:
        greet(z_peer(k))
    greet(peer_x)

    @pl.when(has_up)
    def _():
        greet((grp, dom - 1))
        greet((z * 2 + xo, dom - 1))

    @pl.when(has_down)
    def _():
        greet((grp, dom + 1))
        greet((z * 2 + xo, dom + 1))

    sub = lax.broadcasted_iota(jnp.int32, (8, 128), 0)
    lane = lax.broadcasted_iota(jnp.int32, (8, 128), 1)
    zero = jnp.zeros((8, 128), jnp.float32)

    @pl.when(dom == 0)
    def _():
        D[0:5] = jnp.zeros((5, 18, 8, 128), jnp.float32)
        K[0:4] = jnp.zeros((4, 18, 8, 128), jnp.float32)
        V[0:4] = jnp.zeros((4, 18, 8, 128), jnp.float32)

    @pl.when(dom == DOM - 1)
    def _():
        D[13:17] = jnp.zeros((4, 18, 8, 128), jnp.float32)
        K[12:15] = jnp.zeros((3, 18, 8, 128), jnp.float32)
        V[12:15] = jnp.zeros((3, 18, 8, 128), jnp.float32)

    def halo(direction, array, c):
        lo, hi = EDGES[c]
        ref = (D, K, V)[array]
        if direction == 0:
            src, dst, n = (8, 0, 5) if array == 0 else (8, 0, 4)
            to = (grp, dom + 1)
        else:
            src, dst, n = (5, 13, 4) if array == 0 else (4, 12, 3)
            to = (grp, dom - 1)
        return pltpu.make_async_remote_copy(
            src_ref=ref.at[pl.ds(src, n), pl.ds(lo, hi - lo)],
            dst_ref=ref.at[pl.ds(dst, n), pl.ds(lo, hi - lo)],
            send_sem=halo_send.at[direction, array, c],
            recv_sem=halo_recv.at[direction, array, c],
            device_id=to,
            device_id_type=MESH,
        )

    def spread(c):
        for source, ref, first in ((in_d, D, 5), (in_k, K, 4), (in_v, V, 4)):
            for e in range(*EDGES[c]):
                for r in range(8):
                    a = (e - 1) % 16
                    tile = source[pl.ds(a * 8 + r, 8, stride=128), :]
                    if e == 0:
                        tile = jnp.where(sub == 0, zero, pltpu.roll(tile, 1, 0))
                    if e == 17:
                        tile = jnp.where(sub == 7, zero, pltpu.roll(tile, 7, 0))
                    ref[first + r, e] = tile

    for load in loads:
        load.wait()
    for c in range(CHUNKS):
        spread(c)
        if c == 0:
            pl.semaphore_wait(
                barrier,
                Z + 2 * has_up.astype(jnp.int32) + 2 * has_down.astype(jnp.int32),
            )

        @pl.when(has_down)
        def _():
            for array in range(3):
                halo(0, array, c).start()

        @pl.when(has_up)
        def _():
            for array in range(3):
                halo(1, array, c).start()

    level = lev_ref[0]
    coef = coef_ref[0].astype(jnp.float32)
    keep = [
        jnp.minimum(jnp.maximum(level - (finest - 1), 0), 1).astype(jnp.float32)
        for finest in (6, 7, 8)
    ]

    def step(src, dst, first, last, c, offset, inner):
        for r in range(first, last + 1):
            mid = [src[r + 5, offset + j] for j in range(6)]
            from_left = [pltpu.roll(t, 1, 1) for t in mid]
            from_right = [pltpu.roll(t, 127, 1) for t in mid]
            for j in inner:
                left = from_left[j]
                right = from_right[j]
                if j > 0:
                    left = jnp.where(lane == 0, from_left[j - 1], left)
                if j < 5:
                    right = jnp.where(lane == 127, from_right[j + 1], right)
                below = src[r + 4, offset + j]
                above = src[r + 6, offset + j]
                dst[r + 5, j] = (
                    mid[j]
                    + K[r + 4, 4 * c + j] * (above + below + right + left - 4.0 * mid[j])
                    - 0.5 * V[r + 4, 4 * c + j] * (above - below)
                )

    def x_send(c):
        return pltpu.make_async_remote_copy(
            src_ref=W.at[c, xo], dst_ref=RX.at[c],
            send_sem=xs.at[c], recv_sem=xr.at[c],
            device_id=peer_x, device_id_type=MESH,
        )

    def z_send(c, k):
        return pltpu.make_async_remote_copy(
            src_ref=PZ.at[c, (z + k) % Z], dst_ref=RZ.at[c, k - 1],
            send_sem=zs.at[c], recv_sem=zr.at[c],
            device_id=z_peer(k), device_id_type=MESH,
        )

    def g_send(c, k):
        return pltpu.make_async_remote_copy(
            src_ref=G.at[c, x, z], dst_ref=G.at[c, x, z],
            send_sem=gs.at[c], recv_sem=gr.at[c],
            device_id=z_peer(k), device_id_type=MESH,
        )

    def xg_send(c):
        return pltpu.make_async_remote_copy(
            src_ref=G.at[c, x], dst_ref=G.at[c, x],
            send_sem=xgs.at[c], recv_sem=xgr.at[c],
            device_id=peer_x, device_id_type=MESH,
        )

    def h_send(c, other):
        return pltpu.make_async_remote_copy(
            src_ref=G.at[c, x, pl.ds(14, 2)], dst_ref=H.at[c, x],
            send_sem=hs.at[c, other], recv_sem=hr.at[c, other],
            device_id=(z * 2 + (xo if other else x), dom + 1), device_id_type=MESH,
        )

    def all_bytes(c, sem):
        return pltpu.make_async_copy(RZ.at[c], RZ.at[c], sem.at[c])

    def advance(c):
        @pl.when(has_up)
        def _():
            for array in range(3):
                halo(0, array, c).wait_recv()

        @pl.when(has_down)
        def _():
            for array in range(3):
                halo(1, array, c).wait_recv()

        every = range(6)
        step(D, A, -4, 10, c, 4 * c, every)
        step(A, B, -3, 9, c, 0, every)
        step(B, A, -2, 8, c, 0, every)
        step(A, B, -1, 7, c, 0, range(1, 5))
        w6, w7, w8 = (coef * k for k in keep)
        for a in range(4):
            s = [B[r + 5, a + 1] for r in range(-1, 8)]
            prev, s = s[0], s[1:]
            weighted = [
                w8 * (s[0] - 0.5 * (prev + s[1])),
                w7 * (s[1] - 0.5 * (prev + s[3])),
                w8 * (s[2] - 0.5 * (s[1] + s[3])),
                w6 * (s[3] - 0.5 * (prev + s[7])),
                w8 * (s[4] - 0.5 * (s[3] + s[5])),
                w7 * (s[5] - 0.5 * (s[3] + s[7])),
                w8 * (s[6] - 0.5 * (s[5] + s[7])),
                coef * s[7],
            ]
            for r in range(8):
                W[c, a // 2, 2 * r + a % 2] = weighted[r]
        x_send(c).start()

    def pair_sum(c):
        x_send(c).wait_recv()
        for p in range(16):
            PZ[c, p] = W[c, x, p] + RX[c, p]
        for k in FAR_FIRST:
            z_send(c, k).start()

    def ring_sum(c):
        all_bytes(c, zr).wait()
        total = PZ[c, z]
        for k in range(15):
            total = total + RZ[c, k]
        G[c, x, z] = total
        for k in FAR_FIRST:
            g_send(c, k).start()

    def share(c):
        all_bytes(c, gr).wait()
        xg_send(c).start()

        @pl.when(has_down)
        def _():
            h_send(c, 0).start()
            h_send(c, 1).start()

    def nodal(c):
        xg_send(c).wait_recv()

        @pl.when(has_up)
        def _():
            h_send(c, 0).wait_recv()
            h_send(c, 1).wait_recv()

        m6, m7, m8 = keep
        for a in range(4):
            t = [G[c, a // 2, 2 * r + a % 2] for r in range(8)]
            prev = H[c, a // 2, a % 2]
            o7 = t[7]
            o3 = 0.5 * (prev + o7) + m6 * t[3]
            o1 = 0.5 * (prev + o3) + m7 * t[1]
            o5 = 0.5 * (o3 + o7) + m7 * t[5]
            o0 = 0.5 * (prev + o1) + m8 * t[0]
            o2 = 0.5 * (o1 + o3) + m8 * t[2]
            o4 = 0.5 * (o3 + o5) + m8 * t[4]
            o6 = 0.5 * (o5 + o7) + m8 * t[6]
            for r, o in enumerate((o0, o1, o2, o3, o4, o5, o6, o7)):
                out_ref[pl.ds((4 * c + a) * 8 + r, 8, stride=128), :] = o

    @pl.when(dom == 0)
    def _():
        H[...] = jnp.zeros((CHUNKS, 2, 2, 8, 128), jnp.float32)

    for stage, c in (
        (advance, 0), (advance, 1), (pair_sum, 0), (advance, 2), (pair_sum, 1), (advance, 3), (pair_sum, 2),
        (ring_sum, 0), (pair_sum, 3), (ring_sum, 1), (share, 0), (ring_sum, 2), (share, 1), (nodal, 0),
        (ring_sum, 3), (share, 2), (nodal, 1), (share, 3), (nodal, 2), (nodal, 3),
    ):
        stage(c)

    for c in range(CHUNKS):
        x_send(c).wait_send()
        all_bytes(c, zs).wait()
        all_bytes(c, gs).wait()
        xg_send(c).wait_send()

        @pl.when(has_down)
        def _():
            for array in range(3):
                halo(0, array, c).wait_send()
            h_send(c, 0).wait_send()
            h_send(c, 1).wait_send()

        @pl.when(has_up)
        def _():
            for array in range(3):
                halo(1, array, c).wait_send()


def on_device(density, diffusion, drift_speed, levels, coefficient):
    def tiles(block):
        return block.reshape(8, 128, 128).transpose(1, 0, 2).reshape(1024, 128)

    f32 = jnp.float32
    out = pl.pallas_call(
        kernel,
        out_shape=jax.ShapeDtypeStruct((1024, 128), f32),
        in_specs=[pl.BlockSpec(memory_space=pltpu.SMEM)] * 2 + [pl.BlockSpec(memory_space=pl.ANY)] * 3,
        out_specs=pl.BlockSpec(memory_space=pltpu.VMEM),
        scratch_shapes=[
            pltpu.VMEM((1024, 128), f32),
            pltpu.VMEM((1024, 128), f32),
            pltpu.VMEM((1024, 128), f32),
            pltpu.VMEM((17, 18, 8, 128), f32),
            pltpu.VMEM((15, 18, 8, 128), f32),
            pltpu.VMEM((15, 18, 8, 128), f32),
            pltpu.VMEM((17, 6, 8, 128), f32),
            pltpu.VMEM((17, 6, 8, 128), f32),
            pltpu.VMEM((CHUNKS, 2, 16, 8, 128), f32),
            pltpu.VMEM((CHUNKS, 16, 8, 128), f32),
            pltpu.VMEM((CHUNKS, 16, 8, 128), f32),
            pltpu.VMEM((CHUNKS, 15, 8, 128), f32),
            pltpu.VMEM((CHUNKS, 2, 16, 8, 128), f32),
            pltpu.VMEM((CHUNKS, 2, 2, 8, 128), f32),
            pltpu.SemaphoreType.DMA((3,)),
            pltpu.SemaphoreType.DMA((2, 3, CHUNKS)),
            pltpu.SemaphoreType.DMA((2, 3, CHUNKS)),
            pltpu.SemaphoreType.DMA((CHUNKS,)),
            pltpu.SemaphoreType.DMA((CHUNKS,)),
            pltpu.SemaphoreType.DMA((CHUNKS,)),
            pltpu.SemaphoreType.DMA((CHUNKS,)),
            pltpu.SemaphoreType.DMA((CHUNKS,)),
            pltpu.SemaphoreType.DMA((CHUNKS,)),
            pltpu.SemaphoreType.DMA((CHUNKS,)),
            pltpu.SemaphoreType.DMA((CHUNKS,)),
            pltpu.SemaphoreType.DMA((CHUNKS, 2)),
            pltpu.SemaphoreType.DMA((CHUNKS, 2)),
        ],
        compiler_params=pltpu.CompilerParams(collective_id=0, has_side_effects=True),
        name="combine",
    )(levels, coefficient, tiles(density[0]), tiles(diffusion[0]), tiles(drift_speed[0]))
    return out.reshape(128, 8, 128).transpose(1, 0, 2).reshape(1, 8, 16384)


def solution(mesh):
    return jax.shard_map(
        on_device,
        mesh=mesh,
        in_specs=(
            P("grp", "dom", None),
            P("grp", "dom", None),
            P("grp", "dom", None),
            P("grp"),
            P("grp"),
        ),
        out_specs=P("grp", "dom", None),
        check_vma=False,
    )
```

time: 399 us -> 73.4 us (0.18)
  waiting for transfers between devices: 273 us -> 0 us
  Pallas kernels: 0 us -> 70 us
  blocking collectives: 49.2 us -> 0 us
  starting transfers between devices: 48.2 us -> 0 us
  between operations: 14.9 us -> 1.3 us
  other arithmetic: 6.23 us -> 0 us
    psum x1 -> x0, waiting for transfers between devices: 251 us -> none  [on_device(): total = lax.psum(weighted, 'grp')]
    pallas_call x0 -> x1, Pallas kernels: none -> 70 us  [on_device(): pl.pallas_call(kernel, out_shape=jax.ShapeDtypeStruct((1024, 128), f32),...]
    all_to_all x1 -> x0, blocking collectives: 49.2 us -> none  [on_device(): lax.all_to_all(nodal, 'dom', split_axis=0, concat_axis=1, tiled=True)]
    ppermute x8 -> x0, starting transfers between devices: 36.5 us -> none  [the longest x4 21.9 us: extended(): after = lax.ppermute(leading, axis, down)]
    all_to_all x1 -> x0, waiting for transfers between devices: 16.7 us -> none  [on_device(): lax.all_to_all(state, 'dom', split_axis=1, concat_axis=0, tiled=True)]
    all_to_all x1 -> x0, starting transfers between devices: 11.6 us -> none  [on_device(): lax.all_to_all(state, 'dom', split_axis=1, concat_axis=0, tiled=True)]
    ppermute x8 -> x0, waiting for transfers between devices: 5.22 us -> none  [the longest x4 5.2 us: extended(): before = lax.ppermute(last, axis, up)]
  transfers between devices with their start and end apart: 10 -> 0, of which waited for: 6 -> 0; matrix products, arithmetic and copies ran while one was open for 0% -> 0% of each run, Pallas kernels for 0% -> 0%
where the time goes in v1:
time: 73.4 us; the launch traced here: 73.1 us
  Pallas kernels  70 us (95%)
  local copies, waits for them, and re-layouts  1.87 us (3%)
  between operations  1.3 us (2%)
    pallas_call x1, Pallas kernels, on_device(): pl.pallas_call(kernel, out_shape=jax.ShapeDtypeStruct((1024, 128), f32),...  70 us
    unnamed x1, local copies, waits for them, and re-layouts  1.87 us

profile of v1, /device:TPU:1, one launch (start us, length us, event | category | flops | bytes accessed | tf_op | source)
XLA Modules:
  0.0 73.1 jit_solution(8919838874804160620)
XLA Ops:
  1.3 70.0 %combine.1 = f32[1024,128]{1,0:T(8,128)} custom-call(s32[1]{0:T(128)S(6)} %copy.7.lev_ref, s32[1]{0:T(128)S(6)} %copy.8.coef_ref, f32[1024,128]{1,0:T(8,128)} %bitcast.21, f32[1024,128]{1,0:T(8,128)} %bitcast.22, f32[1024,128]{1,0:T(8,128)} %bitcast.23), custom_call_target="tpu_custom_call" | custom-call | tf_op jit(solution)/shard_map/combine/pallas_call | solution.py:307
  71.3 1.9 %copy.9 = f32[1,8,16384]{2,1,0:T(8,128)} copy(f32[1,8,16384]{2,1,0:T(8,128)} %bitcast.20) | data formatting | bytes 1048576

commit v2 on v1

--- a/solution.py
+++ b/solution.py
@@ -16,7 +16,7 @@
 def kernel(
     lev_ref, coef_ref, den_ref, dif_ref, dri_ref, out_ref,
     in_d, in_k, in_v, D, K, V, A, B, W, RX, PZ, RZ, G, H,
-    load_sem, halo_send, halo_recv, xs, xr, zs, zr, gs, gr, xgs, xgr, hs, hr,
+    load_sem, halo_send, halo_recv, chain_sem, open_sem, xs, xr, zs, zr, gs, gr, xgs, xgr, hs, hr,
 ):
     grp = lax.axis_index("grp")
     dom = lax.axis_index("dom")
@@ -28,7 +28,7 @@
     peer_x = (z * 2 + xo, dom)
 
     def z_peer(k):
-        return (((z + k) % Z) * 2 + x, dom)
+        return (((z + k + Z) % Z) * 2 + x, dom)
 
     loads = [
         pltpu.make_async_copy(src, dst, load_sem.at[i])
@@ -42,9 +42,15 @@
     def greet(device):
         pl.semaphore_signal(barrier, inc=1, device_id=device, device_id_type=MESH)
 
-    for k in FAR_FIRST:
-        greet(z_peer(k))
     greet(peer_x)
+
+    @pl.when(z > 0)
+    def _():
+        greet(z_peer(-1))
+
+    @pl.when(z < Z - 1)
+    def _():
+        greet(z_peer(1))
 
     @pl.when(has_up)
     def _():
@@ -109,7 +115,8 @@
         if c == 0:
             pl.semaphore_wait(
                 barrier,
-                Z + 2 * has_up.astype(jnp.int32) + 2 * has_down.astype(jnp.int32),
+                1 + (z > 0).astype(jnp.int32) + (z < Z - 1).astype(jnp.int32)
+                + 2 * has_up.astype(jnp.int32) + 2 * has_down.astype(jnp.int32),
             )
 
         @pl.when(has_down)
@@ -121,6 +128,19 @@
         def _():
             for array in range(3):
                 halo(1, array, c).start()
+
+    @pl.when(z > 0)
+    def _():
+        pl.semaphore_wait(chain_sem, 1)
+
+    @pl.when(z < Z - 1)
+    def _():
+        pl.semaphore_signal(chain_sem, inc=1, device_id=z_peer(1), device_id_type=MESH)
+
+    @pl.when(z == Z - 1)
+    def _():
+        for k in FAR_FIRST:
+            pl.semaphore_signal(open_sem, inc=1, device_id=z_peer(k), device_id_type=MESH)
 
     level = lev_ref[0]
     coef = coef_ref[0].astype(jnp.float32)
@@ -177,11 +197,11 @@
             device_id=peer_x, device_id_type=MESH,
         )
 
-    def h_send(c, other):
+    def h_send(c, cross):
         return pltpu.make_async_remote_copy(
             src_ref=G.at[c, x, pl.ds(14, 2)], dst_ref=H.at[c, x],
-            send_sem=hs.at[c, other], recv_sem=hr.at[c, other],
-            device_id=(z * 2 + (xo if other else x), dom + 1), device_id_type=MESH,
+            send_sem=hs.at[c, cross], recv_sem=hr.at[c, cross],
+            device_id=(z * 2 + (xo if cross else x), dom + 1), device_id_type=MESH,
         )
 
     def all_bytes(c, sem):
@@ -225,6 +245,12 @@
         x_send(c).wait_recv()
         for p in range(16):
             PZ[c, p] = W[c, x, p] + RX[c, p]
+        if c == 0:
+
+            @pl.when(z < Z - 1)
+            def _():
+                pl.semaphore_wait(open_sem, 1)
+
         for k in FAR_FIRST:
             z_send(c, k).start()
 
@@ -275,8 +301,8 @@
 
     for stage, c in (
         (advance, 0), (advance, 1), (pair_sum, 0), (advance, 2), (pair_sum, 1), (advance, 3), (pair_sum, 2),
-        (ring_sum, 0), (pair_sum, 3), (ring_sum, 1), (share, 0), (ring_sum, 2), (share, 1), (nodal, 0),
-        (ring_sum, 3), (share, 2), (nodal, 1), (share, 3), (nodal, 2), (nodal, 3),
+        (ring_sum, 0), (pair_sum, 3), (ring_sum, 1), (ring_sum, 2), (share, 0), (ring_sum, 3), (share, 1),
+        (nodal, 0), (share, 2), (nodal, 1), (share, 3), (nodal, 2), (nodal, 3),
     ):
         stage(c)
 
@@ -327,6 +353,8 @@
             pltpu.SemaphoreType.DMA((3,)),
             pltpu.SemaphoreType.DMA((2, 3, CHUNKS)),
             pltpu.SemaphoreType.DMA((2, 3, CHUNKS)),
+            pltpu.SemaphoreType.REGULAR,
+            pltpu.SemaphoreType.REGULAR,
             pltpu.SemaphoreType.DMA((CHUNKS,)),
             pltpu.SemaphoreType.DMA((CHUNKS,)),
             pltpu.SemaphoreType.DMA((CHUNKS,)),
@@ -338,7 +366,7 @@
             pltpu.SemaphoreType.DMA((CHUNKS, 2)),
             pltpu.SemaphoreType.DMA((CHUNKS, 2)),
         ],
-        compiler_params=pltpu.CompilerParams(collective_id=0, has_side_effects=True),
+        compiler_params=pltpu.CompilerParams(collective_id=0, has_side_effects=True, vmem_limit_bytes=54500 * 1024),
         name="combine",
     )(levels, coefficient, tiles(density[0]), tiles(diffusion[0]), tiles(drift_speed[0]))
     return out.reshape(128, 8, 128).transpose(1, 0, 2).reshape(1, 8, 16384)

time: 73.4 us -> 69.9 us (0.952)
  Pallas kernels: 70 us -> 67.6 us
  local copies, waits for them, and re-layouts: 1.87 us -> 0.8 us
    pallas_call x1, Pallas kernels: 70 us -> 67.6 us  [on_device(): pl.pallas_call(kernel, out_shape=jax.ShapeDtypeStruct((1024, 128), f32),...]
    unnamed x1, local copies, waits for them, and re-layouts: 1.87 us -> 0.8 us
where the time goes in v2:
time: 69.9 us; the launch traced here: 69.7 us
  Pallas kernels  67.6 us (97%)
  between operations  1.3 us (2%)
  local copies, waits for them, and re-layouts  0.8 us (1%)
    pallas_call x1, Pallas kernels, on_device(): pl.pallas_call(kernel, out_shape=jax.ShapeDtypeStruct((1024, 128), f32),...  67.6 us

profile of v2, /device:TPU:1, one launch (start us, length us, event | category | flops | bytes accessed | tf_op | source)
XLA Modules:
  0.0 69.7 jit_solution(6203801840924828459)
XLA Ops:
  1.3 67.6 %combine.1 = f32[1024,128]{1,0:T(8,128)S(1)} custom-call(s32[1]{0:T(128)S(6)} %copy.7.lev_ref, s32[1]{0:T(128)S(6)} %copy.8.coef_ref, f32[1024,128]{1,0:T(8,128)} %bitcast.21, f32[1024,128]{1,0:T(8,128)} %bitcast.22, f32[1024,128]{1,0:T(8,128)} %bitcast.23), custom_call_target="tpu_custom_call" | custom-call | tf_op jit(solution)/shard_map/combine/pallas_call | solution.py:333
  68.9 0.8 %copy.9 = f32[1,8,16384]{2,1,0:T(8,128)} copy(f32[1,8,16384]{2,1,0:T(8,128)S(1)} %bitcast.20) | data formatting | bytes 1048576

commit v3 on v2

--- a/solution.py
+++ b/solution.py
@@ -16,7 +16,7 @@
 def kernel(
     lev_ref, coef_ref, den_ref, dif_ref, dri_ref, out_ref,
     in_d, in_k, in_v, D, K, V, A, B, W, RX, PZ, RZ, G, H,
-    load_sem, halo_send, halo_recv, chain_sem, open_sem, xs, xr, zs, zr, gs, gr, xgs, xgr, hs, hr,
+    load_sem, halo_send, halo_recv, chain_sem, open_sem, first_sem, late_sem, xs, xr, zs, zr, gs, gr, xgs, xgr, hs, hr,
 ):
     grp = lax.axis_index("grp")
     dom = lax.axis_index("dom")
@@ -48,7 +48,7 @@
     def _():
         greet(z_peer(-1))
 
-    @pl.when(z < Z - 1)
+    @pl.when((z > 0) & (z < Z - 1))
     def _():
         greet(z_peer(1))
 
@@ -108,6 +108,25 @@
                         tile = jnp.where(sub == 7, zero, pltpu.roll(tile, 7, 0))
                     ref[first + r, e] = tile
 
+    def pass_token():
+        @pl.when(z == 0)
+        def _():
+            pl.semaphore_signal(first_sem, inc=1, device_id=z_peer(1), device_id_type=MESH)
+
+        @pl.when(z > 1)
+        def _():
+            pl.semaphore_wait(chain_sem, 1)
+
+        @pl.when((z > 0) & (z < Z - 1))
+        def _():
+            pl.semaphore_signal(chain_sem, inc=1, device_id=z_peer(1), device_id_type=MESH)
+
+        @pl.when(z == Z - 1)
+        def _():
+            for k in FAR_FIRST:
+                if k != 1:
+                    pl.semaphore_signal(open_sem, inc=1, device_id=z_peer(k), device_id_type=MESH)
+
     for load in loads:
         load.wait()
     for c in range(CHUNKS):
@@ -115,7 +134,7 @@
         if c == 0:
             pl.semaphore_wait(
                 barrier,
-                1 + (z > 0).astype(jnp.int32) + (z < Z - 1).astype(jnp.int32)
+                1 + (z > 1).astype(jnp.int32) + (z < Z - 1).astype(jnp.int32)
                 + 2 * has_up.astype(jnp.int32) + 2 * has_down.astype(jnp.int32),
             )
 
@@ -129,18 +148,25 @@
             for array in range(3):
                 halo(1, array, c).start()
 
-    @pl.when(z > 0)
-    def _():
-        pl.semaphore_wait(chain_sem, 1)
-
-    @pl.when(z < Z - 1)
-    def _():
-        pl.semaphore_signal(chain_sem, inc=1, device_id=z_peer(1), device_id_type=MESH)
-
-    @pl.when(z == Z - 1)
-    def _():
-        for k in FAR_FIRST:
-            pl.semaphore_signal(open_sem, inc=1, device_id=z_peer(k), device_id_type=MESH)
+        if c == 0:
+            pass_token()
+
+    def most_begun():
+        @pl.when(z < Z - 1)
+        def _():
+            pl.semaphore_wait(open_sem, 1)
+
+        @pl.when(z == 1)
+        def _():
+            pl.semaphore_wait(first_sem, 1)
+            pl.semaphore_signal(open_sem, inc=1, device_id=z_peer(-1), device_id_type=MESH)
+            for k in range(1, Z - 1):
+                pl.semaphore_signal(late_sem, inc=1, device_id=z_peer(k), device_id_type=MESH)
+
+    def first_begun():
+        @pl.when(z > 1)
+        def _():
+            pl.semaphore_wait(late_sem, 1)
 
     level = lev_ref[0]
     coef = coef_ref[0].astype(jnp.float32)
@@ -181,6 +207,13 @@
             src_ref=PZ.at[c, (z + k) % Z], dst_ref=RZ.at[c, k - 1],
             send_sem=zs.at[c], recv_sem=zr.at[c],
             device_id=z_peer(k), device_id_type=MESH,
+        )
+
+    def z_to_first(c):
+        return pltpu.make_async_remote_copy(
+            src_ref=PZ.at[c, 0], dst_ref=RZ.at[c, Z - 1 - z],
+            send_sem=zs.at[c], recv_sem=zr.at[c],
+            device_id=(x, dom), device_id_type=MESH,
         )
 
     def g_send(c, k):
@@ -246,13 +279,22 @@
         for p in range(16):
             PZ[c, p] = W[c, x, p] + RX[c, p]
         if c == 0:
-
-            @pl.when(z < Z - 1)
+            most_begun()
+        if c == 1:
+            first_begun()
+
+            @pl.when(z > 0)
             def _():
-                pl.semaphore_wait(open_sem, 1)
+                z_to_first(0).start()
 
         for k in FAR_FIRST:
-            z_send(c, k).start()
+            if c > 0:
+                z_send(c, k).start()
+            else:
+
+                @pl.when((z + k) % Z != 0)
+                def _():
+                    z_send(c, k).start()
 
     def ring_sum(c):
         all_bytes(c, zr).wait()
@@ -355,6 +397,8 @@
             pltpu.SemaphoreType.DMA((2, 3, CHUNKS)),
             pltpu.SemaphoreType.REGULAR,
             pltpu.SemaphoreType.REGULAR,
+            pltpu.SemaphoreType.REGULAR,
+            pltpu.SemaphoreType.REGULAR,
             pltpu.SemaphoreType.DMA((CHUNKS,)),
             pltpu.SemaphoreType.DMA((CHUNKS,)),
             pltpu.SemaphoreType.DMA((CHUNKS,)),

time: 69.9 us -> 66.9 us (0.957)
  Pallas kernels: 67.6 us -> 64.6 us
    pallas_call x1, Pallas kernels: 67.6 us -> 64.6 us  [on_device(): pl.pallas_call(kernel, out_shape=jax.ShapeDtypeStruct((1024, 128), f32),...]
where the time goes in v3:
time: 66.9 us; the launch traced here: 66.7 us
  Pallas kernels  64.6 us (97%)
  between operations  1.3 us (2%)
  local copies, waits for them, and re-layouts  0.8 us (1%)
    pallas_call x1, Pallas kernels, on_device(): pl.pallas_call(kernel, out_shape=jax.ShapeDtypeStruct((1024, 128), f32),...  64.6 us

profile of v3, /device:TPU:1, one launch (start us, length us, event | category | flops | bytes accessed | tf_op | source)
XLA Modules:
  0.0 66.7 jit_solution(2551482400406534729)
XLA Ops:
  1.3 64.6 %combine.1 = f32[1024,128]{1,0:T(8,128)S(1)} custom-call(s32[1]{0:T(128)S(6)} %copy.7.lev_ref, s32[1]{0:T(128)S(6)} %copy.8.coef_ref, f32[1024,128]{1,0:T(8,128)} %bitcast.21, f32[1024,128]{1,0:T(8,128)} %bitcast.22, f32[1024,128]{1,0:T(8,128)} %bitcast.23), custom_call_target="tpu_custom_call" | custom-call | tf_op jit(solution)/shard_map/combine/pallas_call | solution.py:375
  65.9 0.8 %copy.9 = f32[1,8,16384]{2,1,0:T(8,128)} copy(f32[1,8,16384]{2,1,0:T(8,128)S(1)} %bitcast.20) | data formatting | bytes 1048576

commit v4 on v3

--- a/solution.py
+++ b/solution.py
@@ -80,6 +80,7 @@
 
     def halo(direction, array, c):
         lo, hi = EDGES[c]
+        hi = min(hi, 17)
         ref = (D, K, V)[array]
         if direction == 0:
             src, dst, n = (8, 0, 5) if array == 0 else (8, 0, 4)
@@ -251,6 +252,10 @@
             for array in range(3):
                 halo(1, array, c).wait_recv()
 
+        if c == CHUNKS - 1:
+            for ref, rows in ((D, (0, 5, 13, 17)), (K, (0, 4, 12, 15)), (V, (0, 4, 12, 15))):
+                for r in (*range(rows[0], rows[1]), *range(rows[2], rows[3])):
+                    ref[r, 17] = jnp.where(sub == 7, zero, pltpu.roll(ref[r, 1], 7, 0))
         every = range(6)
         step(D, A, -4, 10, c, 4 * c, every)
         step(A, B, -3, 9, c, 0, every)

time: 66.9 us -> 66.5 us (level)
  no operation moved by 1% of the time
where the time goes in v4:
time: 66.5 us; the launch traced here: 66.4 us
  Pallas kernels  64.3 us (97%)
  between operations  1.3 us (2%)
  local copies, waits for them, and re-layouts  0.8 us (1%)
    pallas_call x1, Pallas kernels, on_device(): pl.pallas_call(kernel, out_shape=jax.ShapeDtypeStruct((1024, 128), f32),...  64.3 us

profile of v4, /device:TPU:1, one launch (start us, length us, event | category | flops | bytes accessed | tf_op | source)
XLA Modules:
  0.0 66.4 jit_solution(3698846540676575808)
XLA Ops:
  1.3 64.3 %combine.1 = f32[1024,128]{1,0:T(8,128)S(1)} custom-call(s32[1]{0:T(128)S(6)} %copy.7.lev_ref, s32[1]{0:T(128)S(6)} %copy.8.coef_ref, f32[1024,128]{1,0:T(8,128)} %bitcast.21, f32[1024,128]{1,0:T(8,128)} %bitcast.22, f32[1024,128]{1,0:T(8,128)} %bitcast.23), custom_call_target="tpu_custom_call" | custom-call | tf_op jit(solution)/shard_map/combine/pallas_call | solution.py:380
  65.6 0.8 %copy.9 = f32[1,8,16384]{2,1,0:T(8,128)} copy(f32[1,8,16384]{2,1,0:T(8,128)S(1)} %bitcast.20) | data formatting | bytes 1048576
